TPU v7x, 32 devices: a whole 2x2x4 slice. The times are simulated.
32 devices in a mesh: groups: 2 (over y), seq: 8 (over z, x), heads: 2 (over core).
Axes of the slice: x: 2, y: 2, z: 4, core: 2. Of those that a mesh axis runs over, the one named last changes fastest.
Arguments:
- queries: bfloat16 [8192, 16, 128], P(('groups', 'seq'), 'heads'), parts along dimension 0, may hold values from -128 to 128
- keys: bfloat16 [8192, 16, 128], P(('groups', 'seq'), 'heads'), parts along dimension 0, may hold values from -128 to 128
- values: bfloat16 [8192, 16, 128], P(('groups', 'seq'), 'heads'), parts along dimension 0, may hold values from -6 to 6
Outputs:
- attended: bfloat16 [8192, 16, 128], P(('groups', 'seq'), 'heads'), parts along dimension 0
There are 2 independent parts, one for each index of `groups`. A program takes and returns all parts, laid end to end along the dimension named above; each array names one. Nothing has to cross between parts.
All inputs are finite; a program needn't handle non-finite values.
Results may differ from a plain program's by a relative error of at most 0.0055.
Values may be sent and summed in bfloat16 or wider, within the bound.
A program may use at most 128 MiB of HBM per device.

v0:
```python
import math

import jax
import jax.numpy as jnp
from jax import lax
from jax.sharding import PartitionSpec as P

BLOCK = 64


neg_big = -1e30
log_two = math.log(2.0)
sectioned_rows = 512


def passed_along(value, axis, steps):
    count = lax.axis_size(axis)
    initial, last = (max(0, -steps), min(count, count - steps))
    return lax.ppermute(value, axis, [(source, source + steps) for source in range(initial, last)])


def pool_rows(block, factor):
    count = block.shape[0] // factor
    grouped = block.astype(jnp.float32).reshape(count, factor, block.shape[1], block.shape[2])
    return jnp.mean(grouped, axis=1).astype(jnp.bfloat16)


def level_scores(query_block, key_rows, valid, bias, scale):
    scores = jnp.einsum("qhd,khd->hqk", query_block, key_rows, preferred_element_type=jnp.float32)
    return jnp.where(valid[None], scores * scale + bias, neg_big)


def shards(queries, keys, values):
    rows, heads, width = queries.shape
    quad = 4 * BLOCK
    scale = 1.0 / math.sqrt(width)
    first = lax.axis_index("seq") * rows
    own1_k = pool_rows(keys, 2)
    own1_v = pool_rows(values, 2)
    own2_k = pool_rows(keys, 4)
    own2_v = pool_rows(values, 4)
    tail_k, tail_v = passed_along((keys[rows - quad :], values[rows - quad :]), "seq", 1)
    lead = (
        tail_k[quad - BLOCK :],
        tail_v[quad - BLOCK :],
        pool_rows(tail_k[quad - 2 * BLOCK :], 2),
        pool_rows(tail_v[quad - 2 * BLOCK :], 2),
        pool_rows(tail_k, 4),
        pool_rows(tail_v, 4),
    )
    ext0_k = jnp.concatenate([lead[0], keys], 0)
    ext0_v = jnp.concatenate([lead[1], values], 0)
    ext1_k = jnp.concatenate([lead[2], own1_k], 0)
    ext1_v = jnp.concatenate([lead[3], own1_v], 0)
    ext2_k = jnp.concatenate([lead[4], own2_k], 0)
    ext2_v = jnp.concatenate([lead[5], own2_v], 0)

    def one_block(blk):
        local = blk * quad
        start = first + local
        posit = start + jnp.arange(quad, dtype=jnp.int32)
        bound0 = (posit // BLOCK - 1) * BLOCK
        bound1 = (posit // (2 * BLOCK) - 1) * 2 * BLOCK
        bound2 = (posit // quad - 1) * quad
        query_block = lax.dynamic_slice_in_dim(queries, local, quad, 0)
        tokens0 = start - BLOCK + jnp.arange(quad + BLOCK, dtype=jnp.int32)
        rows1 = start // 2 - BLOCK + jnp.arange(quad // 2 + BLOCK, dtype=jnp.int32)
        rows2 = start // 4 - BLOCK + jnp.arange(quad // 4 + BLOCK, dtype=jnp.int32)
        key0 = lax.dynamic_slice_in_dim(ext0_k, local, quad + BLOCK, 0)
        val0 = lax.dynamic_slice_in_dim(ext0_v, local, quad + BLOCK, 0)
        key1 = lax.dynamic_slice_in_dim(ext1_k, local // 2, quad // 2 + BLOCK, 0)
        val1 = lax.dynamic_slice_in_dim(ext1_v, local // 2, quad // 2 + BLOCK, 0)
        key2 = lax.dynamic_slice_in_dim(ext2_k, local // 4, quad // 4 + BLOCK, 0)
        val2 = lax.dynamic_slice_in_dim(ext2_v, local // 4, quad // 4 + BLOCK, 0)
        valid0 = (
            (tokens0 >= 0)[None]
            & (tokens0[None] >= bound0[:, None])
            & (tokens0[None] <= posit[:, None])
        )
        valid1 = (
            (rows1 >= 0)[None]
            & (2 * rows1[None] >= bound1[:, None])
            & (2 * rows1[None] + 2 <= bound0[:, None])
        )
        valid2 = (
            (rows2 >= 0)[None]
            & (4 * rows2[None] >= bound2[:, None])
            & (4 * rows2[None] + 4 <= bound1[:, None])
        )
        scores = jnp.concatenate(
            [
                level_scores(query_block, key0, valid0, 0.0, scale),
                level_scores(query_block, key1, valid1, log_two, scale),
                level_scores(query_block, key2, valid2, 2.0 * log_two, scale),
            ],
            axis=2,
        )
        value_rows = jnp.concatenate([val0, val1, val2], 0)
        top = jnp.max(scores, axis=2)
        weights = jnp.exp(scores - top[..., None])
        total = jnp.sum(weights, axis=2)
        summed = jnp.einsum(
            "hqk,khd->hqd",
            weights.astype(jnp.bfloat16),
            value_rows,
            preferred_element_type=jnp.float32,
        )
        return (top, total, summed)

    tops, totals, sums = lax.map(one_block, jnp.arange(rows // quad, dtype=jnp.int32))
    top = tops.transpose(1, 0, 2).reshape(heads, rows)
    total = totals.transpose(1, 0, 2).reshape(heads, rows)
    summed = sums.transpose(1, 0, 2, 3).reshape(heads, rows, width)
    positions = first + jnp.arange(rows, dtype=jnp.int32)
    bound_far = (positions // quad - 1) * quad
    bound_last = bound_far[rows - 1]
    beyond = rows * lax.axis_size("seq")
    coarse_k = pool_rows(keys, 8)
    coarse_v = pool_rows(values, 8)

    def attend(inner, block_k, block_v, block_rows):

        def work(state):
            best, weight_sum, accum = state
            valid = 8 * block_rows[None] + 8 <= bound_far[:, None]
            scores = level_scores(queries, block_k, valid, 3.0 * log_two, scale)
            fresh = jnp.maximum(best, jnp.max(scores, axis=2))
            fade = jnp.exp(best - fresh)
            weights = jnp.exp(scores - fresh[..., None])
            weight_sum = weight_sum * fade + jnp.sum(weights, axis=2)
            accum = accum * fade[..., None] + jnp.einsum(
                "hqk,khd->hqd",
                weights.astype(jnp.bfloat16),
                block_v,
                preferred_element_type=jnp.float32,
            )
            return (fresh, weight_sum, accum)

        lowest = jnp.min(block_rows)
        return lax.cond(8 * lowest + 8 <= bound_last, work, lambda state: state, inner)

    def absorb(carry, piece):
        best, weight_sum, accum, section_k, section_v, section_rows, fill = carry
        piece_k, piece_v = piece
        count = piece_k.shape[0]
        piece_rows = jnp.arange(count, dtype=jnp.int32)
        if count > sectioned_rows:
            width_sub = max((size for size in range(1, sectioned_rows + 1) if count % size == 0))
            split_k = piece_k.reshape(count // width_sub, width_sub, heads, width)
            split_v = piece_v.reshape(count // width_sub, width_sub, heads, width)
            split_rows = piece_rows.reshape(count // width_sub, width_sub)

            def step(state, item):
                return (attend(state, item[0], item[1], item[2]), None)

            inner, unused = lax.scan(
                step, (best, weight_sum, accum), (split_k, split_v, split_rows)
            )
            best, weight_sum, accum = inner
            return (best, weight_sum, accum, section_k, section_v, section_rows, fill)
        section_k = lax.dynamic_update_slice_in_dim(section_k, piece_k, fill, 0)
        section_v = lax.dynamic_update_slice_in_dim(section_v, piece_v, fill, 0)
        section_rows = lax.dynamic_update_slice_in_dim(section_rows, piece_rows, fill, 0)
        fill = fill + count

        def flush(state):
            best, weight_sum, accum, section_k, section_v, section_rows, fill = state
            best, weight_sum, accum = attend(
                (best, weight_sum, accum),
                section_k[:sectioned_rows],
                section_v[:sectioned_rows],
                section_rows[:sectioned_rows],
            )
            blank = jnp.zeros((sectioned_rows, heads, width), jnp.bfloat16)
            section_k = jnp.concatenate([section_k[sectioned_rows:], blank], 0)
            section_v = jnp.concatenate([section_v[sectioned_rows:], blank], 0)
            section_rows = jnp.concatenate(
                [section_rows[sectioned_rows:], jnp.full((sectioned_rows,), beyond, jnp.int32)], 0
            )
            return (
                best,
                weight_sum,
                accum,
                section_k,
                section_v,
                section_rows,
                fill - sectioned_rows,
            )

        return lax.cond(
            fill >= sectioned_rows,
            flush,
            lambda state: state,
            (best, weight_sum, accum, section_k, section_v, section_rows, fill),
        )

    empty_section = jnp.zeros((2 * sectioned_rows, heads, width), jnp.bfloat16)
    section_init = jnp.full((2 * sectioned_rows,), beyond, jnp.int32)
    init = (
        top,
        total,
        summed,
        empty_section,
        empty_section,
        section_init,
        jnp.zeros((), jnp.int32),
    )
    result = absorb(
        init,
        (
            lax.all_gather(coarse_k, "seq", axis=0, tiled=True),
            lax.all_gather(coarse_v, "seq", axis=0, tiled=True),
        ),
    )
    top, total, summed, section_k, section_v, section_rows, fill = result
    top, total, summed = attend(
        (top, total, summed),
        section_k[:sectioned_rows],
        section_v[:sectioned_rows],
        section_rows[:sectioned_rows],
    )
    return (summed / total[..., None]).transpose(1, 0, 2).astype(jnp.bfloat16)


def solution(mesh):
    return jax.shard_map(
        shards,
        mesh=mesh,
        in_specs=(
            P(("groups", "seq"), "heads", None),
            P(("groups", "seq"), "heads", None),
            P(("groups", "seq"), "heads", None),
        ),
        out_specs=P(("groups", "seq"), "heads", None),
        check_vma=False,
    )
```

profile of v0, /device:TPU:28, one launch (start us, length us, event | category | flops | bytes accessed | tf_op | source)
XLA Modules:
  0.0 123.1 jit_solution(372660217673981330)
XLA Ops:
  11.1 3.5 %collective-permute-start = (bf16[256,8,128]{2,0,1:T(8,128)(2,1)}, bf16[256,8,128]{2,0,1:T(8,128)(2,1)}, u32[]{:S(2)}, u32[]{:S(2)}) collective-permute-start(bf16[256,8,128]{2,0,1:T(8,128)(2,1)} %slice.36), channel_id=1, source_target_pairs={{0,2},{2,4},{4,6},{6,8},{8,10},{10,12},{12,14},{1,3},{3,5},{5,7},{... | collective-permute-start | bytes 1572872 | tf_op jit(solution)/shard_map/ppermute | solution.py:19
  15.7 1.9 %collective-permute-start.1 = (bf16[256,8,128]{2,0,1:T(8,128)(2,1)}, bf16[256,8,128]{2,0,1:T(8,128)(2,1)}, u32[]{:S(2)}, u32[]{:S(2)}) collective-permute-start(bf16[256,8,128]{2,0,1:T(8,128)(2,1)} %slice.39), channel_id=1, source_target_pairs={{0,2},{2,4},{4,6},{6,8},{8,10},{10,12},{12,14},{1,3},{3,5},{5,7},{... | collective-permute-start | bytes 1572872 | tf_op jit(solution)/shard_map/ppermute | solution.py:19
  21.9 2.2 %multiply_convert_fusion.1 = bf16[256,8,128]{2,1,0:T(8,128)(2,1)} fusion(f32[256,8,128]{2,1,0:T(8,128)} %bitcast_reduce_fusion.6), kind=kLoop, calls=%fused_computation.116 | loop fusion | flops 524288 | bytes 1572864 | tf_op jit(solution)/shard_map/convert_element_type | solution.py:25
  24.1 1.9 %multiply_convert_fusion.3 = bf16[128,8,128]{2,1,0:T(8,128)(2,1)} fusion(f32[128,8,128]{2,1,0:T(8,128)} %bitcast_reduce_fusion.5), kind=kLoop, calls=%fused_computation.123 | loop fusion | flops 262144 | bytes 786432 | tf_op jit(solution)/shard_map/convert_element_type | solution.py:25
  28.4 5.0 %collective-permute-done = bf16[256,8,128]{2,0,1:T(8,128)(2,1)} collective-permute-done((bf16[256,8,128]{2,0,1:T(8,128)(2,1)}, bf16[256,8,128]{2,0,1:T(8,128)(2,1)}, u32[]{:S(2)}, u32[]{:S(2)}) %collective-permute-start) | collective-permute-done | bytes 524320 | tf_op jit(solution)/shard_map/ppermute | solution.py:19
  35.4 16.3 %collective-permute-done.1 = bf16[256,8,128]{2,0,1:T(8,128)(2,1)} collective-permute-done((bf16[256,8,128]{2,0,1:T(8,128)(2,1)}, bf16[256,8,128]{2,0,1:T(8,128)(2,1)}, u32[]{:S(2)}, u32[]{:S(2)}) %collective-permute-start.1) | collective-permute-done | bytes 524320 | tf_op jit(solution)/shard_map/ppermute | solution.py:19
  57.4 1.8 %convert_reduce_fusion.1 = f32[64,8,128]{2,0,1:T(8,128)S(1)} fusion(bf16[64,4,8,128]{3,1,0,2:T(4,128)(2,1)} %bitcast.27), kind=kLoop, calls=%fused_computation.114 | loop fusion | flops 458752 | bytes 786432 | tf_op jit(solution)/shard_map/reduce_sum | solution.py:25
  59.3 1.7 %convert_reduce_fusion = f32[64,8,128]{2,0,1:T(8,128)S(1)} fusion(bf16[64,4,8,128]{3,1,0,2:T(4,128)(2,1)} %bitcast.29), kind=kLoop, calls=%fused_computation.113 | loop fusion | flops 458752 | bytes 786432 | tf_op jit(solution)/shard_map/reduce_sum | solution.py:25
  64.7 34.1 %while.17 = (s32[]{:T(128)}, f32[2,8,256]{2,1,0:T(8,128)}, f32[2,8,256]{2,1,0:T(8,128)}, f32[2,8,256,128]{3,2,1,0:T(8,128)}, s32[2]{0:T(128)S(1)}, /*index=5*/s3...) while((s32[]{:T(128)}, f32[2,8,256]{2,1,0:T(8,128)}, ...), condition=%wide.region_13.14_spmd, body=%wide.region_8.13_spmd.sunk | while | flops 690760192 | bytes 39908296 | solution.py:110
  68.5 2.2 %fusion.92 = (f32[8,256]{1,0:T(8,128)}, f32[8,256,192]{1,2,0:T(8,128)}) fusion(bf16[192,8,128]{2,1,0:T(8,128)(2,1)S(1)} %get-tuple-element.547, bf16[256,8,128]{2,1,0:T(8,128)(2,1)S(1)} %constant_dynamic-slice_fusion.11, pred[256,192]{0,1:T(8,128)(4,1)S(1)} %compare_and_fusion.8), kind=kOutput, calls=%fused_computation.145.clone.1 | convolution fusion | flops 102234112 | bytes 2547712 | tf_op jit(solution)/shard_map/while/body/eval_jaxpr/qhd,khd->hqk/dot_general | solution.py:29
  73.2 1.9 %constant_dynamic-slice_fusion.10 = (bf16[128,8,128]{2,1,0:T(8,128)(2,1)}, bf16[128,8,128]{2,1,0:T(8,128)(2,1)}) fusion(bf16[192,8,128]{2,1,0:T(8,128)(2,1)} %get-tuple-element.618, s32[]{:T(128)S(6)} %select_n.189, bf16[192,8,128]{2,1,0:T(8,128)(2,1)} %get-tuple-element.615), kind=kLoop, calls=%fused_computation.29.clone.1 | loop fusion | bytes 1048580 | tf_op jit(solution)/shard_map/while/body/eval_jaxpr/dynamic_slice | solution.py:74
  78.2 2.2 %fusion.94 = f32[2,8,256,128]{3,2,1,0:T(8,128)} fusion(f32[2,8,256,128]{3,2,1,0:T(8,128)} %get-tuple-element.585, s32[]{:T(128)} %get-tuple-element.582, f32[8,256,128]{1,2,0:T(8,128)S(1)} %get-tuple-element.552, f32[8,256,192]{1,2,0:T(8,128)S(1)} %copy-done, f32[8,256,320]{1,2,0:T(8,128)S(1)} %get-tuple-element.554, ...), kind=kOutput, calls=%fused_computation.8.clone.1 | convolution fusion | flops 344719360 | bytes 7610880 | tf_op jit(solution)/shard_map/while/body/eval_jaxpr/hqk,khd->hqd/dot_general | solution.py:102
  85.5 2.2 %fusion.92 = (f32[8,256]{1,0:T(8,128)}, f32[8,256,192]{1,2,0:T(8,128)}) fusion(bf16[192,8,128]{2,1,0:T(8,128)(2,1)S(1)} %get-tuple-element.547, bf16[256,8,128]{2,1,0:T(8,128)(2,1)S(1)} %constant_dynamic-slice_fusion.11, pred[256,192]{0,1:T(8,128)(4,1)S(1)} %compare_and_fusion.8), kind=kOutput, calls=%fused_computation.145.clone.1 | convolution fusion | flops 102234112 | bytes 2547712 | tf_op jit(solution)/shard_map/while/body/eval_jaxpr/qhd,khd->hqk/dot_general | solution.py:29
  88.5 1.6 %fusion.89 = (f32[8,256]{1,0:T(8,128)S(1)}, f32[8,256,320]{1,2,0:T(8,128)S(1)}) fusion(bf16[576,8,128]{2,0,1:T(8,128)(2,1)} %get-tuple-element.613, s32[]{:T(128)S(6)} %select_n.192, bf16[256,8,128]{2,1,0:T(8,128)(2,1)S(1)} %constant_dynamic-slice_fusion.11, pred[256,320]{0,1:T(8,128)(4,1)} %compare_and_fusion.7), kind=kOutput, calls=%fused_computation.144.clone.1 | convolution fusion | flops 169736192 | bytes 3891204 | tf_op jit(solution)/shard_map/while/body/eval_jaxpr/qhd,khd->hqk/dot_general | solution.py:29
  90.2 1.9 %constant_dynamic-slice_fusion.10 = (bf16[128,8,128]{2,1,0:T(8,128)(2,1)}, bf16[128,8,128]{2,1,0:T(8,128)(2,1)}) fusion(bf16[192,8,128]{2,1,0:T(8,128)(2,1)} %get-tuple-element.618, s32[]{:T(128)S(6)} %select_n.189, bf16[192,8,128]{2,1,0:T(8,128)(2,1)} %get-tuple-element.615), kind=kLoop, calls=%fused_computation.29.clone.1 | loop fusion | bytes 1048580 | tf_op jit(solution)/shard_map/while/body/eval_jaxpr/dynamic_slice | solution.py:74
  95.2 2.2 %fusion.94 = f32[2,8,256,128]{3,2,1,0:T(8,128)} fusion(f32[2,8,256,128]{3,2,1,0:T(8,128)} %get-tuple-element.585, s32[]{:T(128)} %get-tuple-element.582, f32[8,256,128]{1,2,0:T(8,128)S(1)} %get-tuple-element.552, f32[8,256,192]{1,2,0:T(8,128)S(1)} %copy-done, f32[8,256,320]{1,2,0:T(8,128)S(1)} %get-tuple-element.554, ...), kind=kOutput, calls=%fused_computation.8.clone.1 | convolution fusion | flops 344719360 | bytes 7610880 | tf_op jit(solution)/shard_map/while/body/eval_jaxpr/hqk,khd->hqd/dot_general | solution.py:102
  98.8 1.8 %copy.52 = f32[8,2,256,128]{3,2,1,0:T(8,128)S(1)} copy(f32[8,2,256,128]{3,2,0,1:T(8,128)} %bitcast.63) | data formatting | bytes 4194304 | tf_op jit(solution)/shard_map/transpose | solution.py:113
  100.7 10.1 %conditional.2 = ((f32[8,512]{1,0:T(8,128)S(1)}, f32[8,512]{1,0:T(8,128)S(1)}, f32[8,512,128]{2,1,0:T(8,128)S(1)})) conditional(s32[]{:T(128)} %bitcast.6, (f32[8,512]{1,0:T(8,128)S(1)}, f32[8,512]{1,0:T(8,128)S(1)}, f32[8,512,128]{2,1,0:T(8,128)S(1)}) %tuple.115, (s32[512]{0:T(512)S(1)}, s32[512]{0:T(512)S(1)}, bf16[512,8,128]{2,1,0:T(8,128)(2,1)}, ...), branch_computations={%region_16.17_spmd, %region_17.20_spmd} | conditional | flops 1104421888 | bytes 38019132 | solution.py:140
  101.1 3.7 %fusion.34 = (f32[8,512]{1,0:T(8,128)S(1)}, f32[8,512,512]{1,2,0:T(8,128)S(1)}) fusion(pred[512,512]{0,1:T(8,128)(4,1)S(1)} %broadcast_compare_fusion.1, bf16[512,8,128]{2,1,0:T(8,128)(2,1)} %get-tuple-element.372, bf16[512,8,128]{2,1,0:T(8,128)(2,1)} %get-tuple-element.371), kind=kOutput, calls=%fused_computation.68 | convolution fusion | flops 545255424 | bytes 10764288 | tf_op jit(solution)/shard_map/cond/branch_1_fun/cond/branch_1_fun/qhd,khd->hqk/dot_general | solution.py:29
  104.9 2.1 %fusion.33 = f32[8,512]{1,0:T(8,128)S(1)} fusion(f32[8,512,512]{1,2,0:T(8,128)S(1)} %get-tuple-element.436, f32[8,512]{1,0:T(8,128)S(1)} %max.5, pred[512,512]{0,1:T(8,128)(4,1)S(1)} %broadcast_compare_fusion.1), kind=kLoop, calls=%fused_computation.67 | loop fusion | flops 10481664 | bytes 8683520 | tf_op jit(solution)/shard_map/cond/branch_1_fun/cond/branch_1_fun/reduce_sum | solution.py:130
  107.0 3.8 %multiply_add_fusion = f32[8,512,128]{2,1,0:T(8,128)S(1)} fusion(f32[8,512,128]{2,1,0:T(8,128)S(1)} %get-tuple-element.281, f32[8,512,512]{1,2,0:T(8,128)S(1)} %get-tuple-element.436, f32[8,512]{1,0:T(8,128)S(1)} %max.5, pred[512,512]{0,1:T(8,128)(4,1)S(1)} %broadcast_compare_fusion.1, bf16[512,8,128]{2,1,0:T(8,128)(2,1)S(1)} %copy-done.16, ...), kind=kOutput, calls=%fused_computation.71 | convolution fusion | flops 548405248 | bytes 13926400 | tf_op jit(solution)/shard_map/cond/branch_1_fun/cond/branch_1_fun/hqk,khd->hqd/dot_general | solution.py:131
  110.8 2.6 %conditional.3 = (f32[8,512]{1,0:T(8,128)S(1)}, f32[8,512,128]{2,0,1:T(8,128)}) conditional(s32[]{:T(128)} %bitcast.5, (f32[8,512]{1,0:T(8,128)S(1)}, f32[8,512,128]{2,1,0:T(8,128)S(1)}) %tuple.43, (s32[512]{0:T(512)S(1)}, bf16[512,8,128]{2,1,0:T(8,128)(2,1)}, f32[8,512]{1,0:T(8,128)S(1)}, f32[8,512]{1,0:T(8,128)S(1)}, ...), branch_computations={%region_20.21_spmd, %region_21.24_spmd} | conditional | flops 1104159232 | bytes 34836496 | solution.py:140
  110.8 2.6 %copy.62 = f32[8,512,128]{2,0,1:T(8,128)} copy(f32[8,512,128]{2,1,0:T(8,128)S(1)} %get-tuple-element.383) | data formatting | bytes 4194304 | tf_op jit(solution)/shard_map/cond | solution.py:140
  113.5 2.7 %fusion.64 = bf16[512,8,128]{2,1,0:T(8,128)(2,1)} fusion(f32[8,512,128]{2,0,1:T(8,128)} %get-tuple-element.384, f32[8,512]{0,1:T(8,128)S(1)} %copy.57), kind=kLoop, calls=%fused_computation.117 | loop fusion | flops 1048576 | bytes 3162112 | tf_op jit(solution)/shard_map/convert_element_type | solution.py:222
  (148 shorter events, 40.8 us)
Async XLA Ops:
  6.5 8.1 %copy-start.4 = (bf16[512,8,128]{2,1,0:T(8,128)(2,1)S(1)}, bf16[512,8,128]{2,1,0:T(8,128)(2,1)}, u32[]{:S(2)}) copy-start(bf16[512,8,128]{2,1,0:T(8,128)(2,1)} %param.11) | copy-start | bytes 3145732
  6.5 94.0 %all-gather.3.cloned.1.call-start = ((), (), s32[]{:S(2)}) async-start(), calls=%async_computation | async-start | bytes 1179648 | tf_op jit(solution)/shard_map/all_gather | solution.py:211
  8.8 91.8 %all-gather.5.cloned.1.call-start = ((), (), s32[]{:S(2)}) async-start(), calls=%async_computation.1 | async-start | bytes 1179648 | tf_op jit(solution)/shard_map/all_gather | solution.py:212
  10.2 7.6 %copy-start.5 = (bf16[512,8,128]{2,0,1:T(8,128)(2,1)}, bf16[512,8,128]{2,0,1:T(8,128)(2,1)S(1)}, u32[]{:S(2)}) copy-start(bf16[512,8,128]{2,0,1:T(8,128)(2,1)S(1)} %copy.39) | copy-start | bytes 3145732
  11.1 7.4 %copy-start.3 = (bf16[512,8,128]{2,1,0:T(8,128)(2,1)S(1)}, bf16[512,8,128]{2,1,0:T(8,128)(2,1)}, u32[]{:S(2)}) copy-start(bf16[512,8,128]{2,1,0:T(8,128)(2,1)} %param.10) | copy-start | bytes 3145732
  11.1 22.2 %collective-permute-start = (bf16[256,8,128]{2,0,1:T(8,128)(2,1)}, bf16[256,8,128]{2,0,1:T(8,128)(2,1)}, u32[]{:S(2)}, u32[]{:S(2)}) collective-permute-start(bf16[256,8,128]{2,0,1:T(8,128)(2,1)} %slice.36), channel_id=1, source_target_pairs={{0,2},{2,4},{4,6},{6,8},{8,10},{10,12},{12,14},{1,3},{3,5},{5,7},{... | collective-permute-start | bytes 1572872 | tf_op jit(solution)/shard_map/ppermute | solution.py:19
  15.7 36.1 %collective-permute-start.1 = (bf16[256,8,128]{2,0,1:T(8,128)(2,1)}, bf16[256,8,128]{2,0,1:T(8,128)(2,1)}, u32[]{:S(2)}, u32[]{:S(2)}) collective-permute-start(bf16[256,8,128]{2,0,1:T(8,128)(2,1)} %slice.39), channel_id=1, source_target_pairs={{0,2},{2,4},{4,6},{6,8},{8,10},{10,12},{12,14},{1,3},{3,5},{5,7},{... | collective-permute-start | bytes 1572872 | tf_op jit(solution)/shard_map/ppermute | solution.py:19
  21.9 4.1 %copy-start.8 = (f32[128,8,128]{2,1,0:T(8,128)S(1)}, f32[128,8,128]{2,1,0:T(8,128)}, u32[]{:S(2)}) copy-start(f32[128,8,128]{2,1,0:T(8,128)} %bitcast_reduce_fusion.3) | copy-start | bytes 1572868
  24.1 10.2 %copy-start.6 = (bf16[512,8,128]{2,0,1:T(8,128)(2,1)S(1)}, bf16[512,8,128]{2,0,1:T(8,128)(2,1)}, u32[]{:S(2)}) copy-start(bf16[512,8,128]{2,0,1:T(8,128)(2,1)} %copy-done.5) | copy-start | bytes 3145732
  26.1 1.9 %copy-start.14 = (s32[512]{0:T(512)}, s32[512]{0:T(512)S(1)}, u32[]{:S(2)}) copy-start(s32[512]{0:T(512)S(1)} %fusion.67) | copy-start | bytes 6148
  55.5 5.7 %copy-start.7 = (bf16[256,8,128]{2,1,0:T(8,128)(2,1)S(1)}, bf16[256,8,128]{2,1,0:T(8,128)(2,1)}, u32[]{:S(2)}) copy-start(bf16[256,8,128]{2,1,0:T(8,128)(2,1)} %multiply_convert_fusion.1) | copy-start | bytes 1572868
  57.4 5.6 %copy-start.9 = (bf16[128,8,128]{2,1,0:T(8,128)(2,1)S(1)}, bf16[128,8,128]{2,1,0:T(8,128)(2,1)}, u32[]{:S(2)}) copy-start(bf16[128,8,128]{2,1,0:T(8,128)(2,1)} %multiply_convert_fusion.3) | copy-start | bytes 786436
  75.0 3.0 %copy-start.1 = (bf16[128,8,128]{2,1,0:T(8,128)(2,1)S(1)}, bf16[128,8,128]{2,1,0:T(8,128)(2,1)}, u32[]{:S(2)}) copy-start(bf16[128,8,128]{2,1,0:T(8,128)(2,1)} %get-tuple-element.556) | copy-start | bytes 786436 | tf_op jit(solution)/shard_map/while
  75.0 3.0 %copy-start.2 = (bf16[576,8,128]{2,0,1:T(8,128)(2,1)S(1)}, bf16[576,8,128]{2,0,1:T(8,128)(2,1)}, u32[]{:S(2)}) copy-start(bf16[576,8,128]{2,0,1:T(8,128)(2,1)} %get-tuple-element.616) | copy-start | bytes 3538948 | tf_op jit(solution)/shard_map/while
  75.0 3.1 %copy-start = (f32[8,256,192]{1,2,0:T(8,128)S(1)}, f32[8,256,192]{1,2,0:T(8,128)}, u32[]{:S(2)}) copy-start(f32[8,256,192]{1,2,0:T(8,128)} %get-tuple-element.553) | copy-start | bytes 4718596 | tf_op jit(solution)/shard_map/while
  80.4 1.4 %copy-start.18 = (s32[2]{0:T(128)S(1)}, s32[2]{0:T(128)}, u32[]{:S(2)}) copy-start(s32[2]{0:T(128)} %copy-done.17) | copy-start | bytes 28 | tf_op jit(solution)/shard_map/while
  92.1 3.0 %copy-start.1 = (bf16[128,8,128]{2,1,0:T(8,128)(2,1)S(1)}, bf16[128,8,128]{2,1,0:T(8,128)(2,1)}, u32[]{:S(2)}) copy-start(bf16[128,8,128]{2,1,0:T(8,128)(2,1)} %get-tuple-element.556) | copy-start | bytes 786436 | tf_op jit(solution)/shard_map/while
  92.1 3.0 %copy-start.2 = (bf16[576,8,128]{2,0,1:T(8,128)(2,1)S(1)}, bf16[576,8,128]{2,0,1:T(8,128)(2,1)}, u32[]{:S(2)}) copy-start(bf16[576,8,128]{2,0,1:T(8,128)(2,1)} %get-tuple-element.616) | copy-start | bytes 3538948 | tf_op jit(solution)/shard_map/while
  92.1 3.1 %copy-start = (f32[8,256,192]{1,2,0:T(8,128)S(1)}, f32[8,256,192]{1,2,0:T(8,128)}, u32[]{:S(2)}) copy-start(f32[8,256,192]{1,2,0:T(8,128)} %get-tuple-element.553) | copy-start | bytes 4718596 | tf_op jit(solution)/shard_map/while
  97.4 1.4 %copy-start.18 = (s32[2]{0:T(128)S(1)}, s32[2]{0:T(128)}, u32[]{:S(2)}) copy-start(s32[2]{0:T(128)} %copy-done.17) | copy-start | bytes 28 | tf_op jit(solution)/shard_map/while
  98.8 1.8 %copy-start.10 = (f32[2,8,256]{2,1,0:T(8,128)S(1)}, f32[2,8,256]{2,1,0:T(8,128)}, u32[]{:S(2)}) copy-start(f32[2,8,256]{2,1,0:T(8,128)} %get-tuple-element.296) | copy-start | bytes 49156
  98.8 1.9 %copy-start.13 = (f32[2,8,256]{2,1,0:T(8,128)S(1)}, f32[2,8,256]{2,1,0:T(8,128)}, u32[]{:S(2)}) copy-start(f32[2,8,256]{2,1,0:T(8,128)} %get-tuple-element.297) | copy-start | bytes 49156
  98.8 1.9 %copy-start.15 = (s32[512]{0:T(512)S(1)}, s32[512]{0:T(512)}, u32[]{:S(2)}) copy-start(s32[512]{0:T(512)} %copy-done.14) | copy-start | bytes 6148
  104.9 2.1 %copy-start.16 = (bf16[512,8,128]{2,1,0:T(8,128)(2,1)S(1)}, bf16[512,8,128]{2,1,0:T(8,128)(2,1)}, u32[]{:S(2)}) copy-start(bf16[512,8,128]{2,1,0:T(8,128)(2,1)} %get-tuple-element.376) | copy-start | bytes 3145732 | tf_op jit(solution)/shard_map/cond/branch_1_fun/cond
  (6 other events, 5.2 us)
Sparse Core Ops, SparseCore 0:
  9.5 43.7 all-gather.2
  55.3 38.9 all-gather.4
where the time goes:
time: 124 us; the launch traced here: 123 us
  other arithmetic  33 us (27%)
  local copies, waits for them, and re-layouts  23.5 us (19%)
  matrix products  22.6 us (18%)
  waiting for transfers between devices  21.4 us (17%)
  between operations  15 us (12%)
  starting transfers between devices  5.47 us (4%)
  loops' own time  2.05 us (2%)
    ppermute x2, waiting for transfers between devices, passed_along(): lax.ppermute(value, axis, [(source, source + steps) for source in range(i...  21.3 us
    dot_general x7, matrix products, level_scores(): jnp.einsum('qhd,khd->hqk', query_block, key_rows, preferred_element_type=...  14.4 us
    reduce_sum x10, other arithmetic, pool_rows(): return jnp.mean(grouped, axis=1).astype(jnp.bfloat16)  10.3 us
    convert_element_type x10, other arithmetic, pool_rows(): return jnp.mean(grouped, axis=1).astype(jnp.bfloat16)  5.6 us
    ppermute x2, starting transfers between devices, passed_along(): lax.ppermute(value, axis, [(source, source + steps) for source in range(i...  5.43 us
    dot_general x2, matrix products, one_block(): jnp.einsum('hqk,khd->hqd', weights.astype(jnp.bfloat16), value_rows, pref...  4.4 us
    dot_general x1, matrix products, work(): jnp.einsum('hqk,khd->hqd', weights.astype(jnp.bfloat16), block_v, preferr...  3.8 us
    dynamic_slice x4, local copies, waits for them, and re-layouts, one_block(): val2 = lax.dynamic_slice_in_dim(ext2_v, local // 4, quad // 4 + BLOCK, 0)  3.8 us
  transfers between devices with their start and end apart: 4, of which 2 were waited for; matrix products, arithmetic and copies ran while one was open for 49% of the time, Pallas kernels for 0%

commit v1 on v0

v1 whole, which is shorter than its diff:
```python
import functools
import math

import jax
import jax.numpy as jnp
from jax import lax
from jax.experimental import pallas as pl
from jax.experimental.pallas import tpu as pltpu
from jax.sharding import PartitionSpec as P

BLOCK = 64
QUAD = 4 * BLOCK
HALF = 2 * BLOCK
NEAR = 5 * BLOCK
NEG = -1e30
F32 = jnp.float32
BF16 = jnp.bfloat16


def to_heads(values, scratch, heads):
    count, _, width = values.shape
    scratch[pl.ds(0, count * heads), :] = values.reshape(count * heads, width)
    return [scratch[pl.ds(h, count, stride=heads), :].astype(BF16) for h in range(heads)]


def halved(values):
    count, heads, width = values.shape
    pairs = values.reshape(count // 2, 2, heads, width)
    return pairs[:, 0] + pairs[:, 1]


def kernel(size, span, q_ref, k_ref, v_ref, o_ref,
           far, tail0, tailp, sendp, eq, e0, e1, e2, fk,
           bias, acc, top, total, tmp, otmp,
           t_send, t_recv, up_send, up_recv, pr_send, pr_recv):
    rows, heads, width = q_ref.shape
    own = rows // 8
    gain = math.log2(math.e) / math.sqrt(width)
    me = lax.axis_index("seq")
    col = lax.rem(me, 2)
    lev = me // 2
    levels = size // 2
    pair = me + 1 - 2 * col
    sources = (k_ref, v_ref)

    barrier = pltpu.get_barrier_semaphore()
    for step in (-2, -1, 1, 2):
        @pl.when((me + step >= 0) & (me + step < size))
        def _():
            pl.semaphore_signal(barrier, inc=1, device_id={"seq": me + step},
                                device_id_type=pl.DeviceIdType.MESH)

    def tail_copy(kv, part, target):
        if part == 0:
            src, dst = sources[kv].at[pl.ds(rows - BLOCK, BLOCK)], tail0.at[kv]
        else:
            src, dst = sendp.at[kv], tailp.at[kv]
        return pltpu.make_async_remote_copy(
            src_ref=src, dst_ref=dst, send_sem=t_send.at[kv, part], recv_sem=t_recv.at[kv, part],
            device_id={"seq": target}, device_id_type=pl.DeviceIdType.MESH)

    def up_copy(kv, b, target):
        return pltpu.make_async_remote_copy(
            src_ref=far.at[kv, b], dst_ref=far.at[kv, b],
            send_sem=up_send.at[kv, b], recv_sem=up_recv.at[kv, b],
            device_id={"seq": target}, device_id_type=pl.DeviceIdType.MESH)

    def pair_copy(kv, b):
        return pltpu.make_async_remote_copy(
            src_ref=far.at[kv, b], dst_ref=far.at[kv, b],
            send_sem=pr_send.at[kv, b], recv_sem=pr_recv.at[kv, b],
            device_id={"seq": pair}, device_id_type=pl.DeviceIdType.MESH)

    climbs = lev < levels - 1
    up = jnp.minimum(me + 2, size - 1)
    after = jnp.minimum(me + 1, size - 1)

    def split(kv, c):
        x = sources[kv][pl.ds(c * BLOCK, BLOCK)].astype(F32)
        two = halved(x)
        four = halved(two)
        eight = halved(four)
        two = two * 0.5
        four = four * 0.25
        far[kv, me, pl.ds(c * 8, 8)] = (eight * 0.125).astype(BF16)
        if c >= rows // BLOCK - 4 and c < rows // BLOCK - 1:
            sendp[kv, pl.ds(32 + 16 * (c - rows // BLOCK + 4), 16)] = four.astype(BF16)
        if c == rows // BLOCK - 2:
            sendp[kv, pl.ds(0, 32)] = two.astype(BF16)

    def spread(kv, c):
        x = sources[kv][pl.ds(c * BLOCK, BLOCK)].astype(F32)
        for h, part in enumerate(to_heads(x, tmp, heads)):
            e0[kv, h, pl.ds(BLOCK + c * BLOCK, BLOCK), :] = part
        if c < rows // BLOCK - 2:
            two = halved(x)
            for h, part in enumerate(to_heads(two * 0.5, tmp, heads)):
                e1[kv, h, pl.ds(BLOCK + c * 32, 32), :] = part
            if c < rows // BLOCK - 4:
                four = halved(two)
                for h, part in enumerate(to_heads(four * 0.25, tmp, heads)):
                    e2[kv, h, pl.ds(BLOCK + c * 16, 16), :] = part

    for kv in range(2):
        for c in range(rows // BLOCK):
            split(kv, c)

    lower = jnp.minimum(me, 2)
    upper = jnp.minimum(size - 1 - me, 2)
    pl.semaphore_wait(barrier, lower + upper)

    for kv in range(2):
        @pl.when(climbs)
        def _():
            up_copy(kv, me, up).start()

        @pl.when(me < size - 1)
        def _():
            tail_copy(kv, 0, after).start()
            tail_copy(kv, 1, after).start()

        @pl.when(col == 0)
        def _():
            pair_copy(kv, me).start()

    for kv in range(2):
        for c in range(rows // BLOCK):
            spread(kv, c)
    for c in range(rows // BLOCK):
        x = q_ref[pl.ds(c * BLOCK, BLOCK)].astype(F32)
        for h, part in enumerate(to_heads(x, tmp, heads)):
            eq[h, pl.ds(c * BLOCK, BLOCK), :] = part

    i = lax.broadcasted_iota(jnp.int32, (HALF, NEAR), 0)
    j = lax.broadcasted_iota(jnp.int32, (HALF, NEAR), 1)
    is0 = j < 192
    is2 = j >= 256
    level = jnp.where(is0, 0.0, jnp.where(is2, 2.0, 1.0))
    ok01 = jnp.where(is0, jnp.where((j <= i + BLOCK) & ((j >= BLOCK) | (i < BLOCK)), 1, 0),
                     jnp.where((j < 224) | (i >= BLOCK), 1, 0))
    for qd in range(rows // QUAD):
        for hf in range(2):
            ok = jnp.where(is2, jnp.where((j < 288) | (hf == 1), 1, 0), ok01)
            if qd == 0:
                real = (j >= BLOCK) & (j < 192) if hf == 0 else j < 256
                ok = jnp.where(real | (me > 0), ok, 0)
            bias[2 * qd + hf] = jnp.where(ok > 0, level, NEG)

    def near(qd):
        def body(h, _):
            for hf in range(2):
                at = qd * QUAD + hf * HALF
                q = eq[h, pl.ds(at, HALF), :]
                kk, vv = (jnp.concatenate([
                    e0[kv, h, pl.ds(at, 192), :],
                    e1[kv, h, pl.ds(at // 2, BLOCK), :],
                    e2[kv, h, pl.ds(qd * BLOCK, BLOCK), :]], 0) for kv in range(2))
                s = lax.dot_general(q, kk, (((1,), (1,)), ((), ())), preferred_element_type=F32)
                s = s * gain + bias[2 * qd + hf]
                m = jnp.max(s, axis=1, keepdims=True)
                w = jnp.exp2(s - m)
                total[h, pl.ds(at, HALF), :] = jnp.sum(w, axis=1, keepdims=True)
                top[h, pl.ds(at, HALF), :] = m
                acc[h, pl.ds(at, HALF), :] = jnp.dot(w.astype(BF16), vv, preferred_element_type=F32)
            return 0
        lax.fori_loop(0, heads, body, 0)

    for qd in range(1, rows // QUAD):
        near(qd)

    def pass_on(r, _):
        b = me - 2 * r
        for kv in range(2):
            up_copy(kv, b, up).wait_recv()

            @pl.when(climbs)
            def _():
                up_copy(kv, b, up).start()

            if kv == 0:
                pair_copy(kv, b).start()
            else:
                @pl.when(col == 1)
                def _():
                    pair_copy(kv, b).start()

        @pl.when(col == 1)
        def _():
            b = me + 1 - 2 * r

            @pl.when(r == 1)
            def _():
                pair_copy(1, b).wait_recv()

            @pl.when(r > 1)
            def _():
                up_copy(1, b, up).wait_recv()

            @pl.when(climbs)
            def _():
                up_copy(1, b, up).start()
        return 0

    def last_even():
        @pl.when(col == 1)
        def _():
            b = me - 1 - 2 * lev

            @pl.when(lev == 0)
            def _():
                pair_copy(1, b).wait_recv()

            @pl.when(lev > 0)
            def _():
                up_copy(1, b, up).wait_recv()

            @pl.when(climbs)
            def _():
                up_copy(1, b, up).start()

    lax.fori_loop(1, lev + 1, pass_on, 0)
    last_even()

    @pl.when(me == 0)
    def _():
        for kv in range(2):
            for h in range(heads):
                e0[kv, h, pl.ds(0, BLOCK), :] = jnp.zeros((BLOCK, width), BF16)
                e1[kv, h, pl.ds(0, BLOCK), :] = jnp.zeros((BLOCK, width), BF16)
                e2[kv, h, pl.ds(0, BLOCK), :] = jnp.zeros((BLOCK, width), BF16)

    @pl.when(me > 0)
    def _():
        for kv in range(2):
            tail_copy(kv, 0, after).wait_recv()
            tail_copy(kv, 1, after).wait_recv()
            x = tail0[kv].astype(F32)
            for h, part in enumerate(to_heads(x, tmp, heads)):
                e0[kv, h, pl.ds(0, BLOCK), :] = part
            two = halved(x)
            four = halved(two)
            for h, part in enumerate(to_heads(two * 0.5, tmp, heads)):
                e1[kv, h, pl.ds(32, 32), :] = part
            for h, part in enumerate(to_heads(four * 0.25, tmp, heads)):
                e2[kv, h, pl.ds(48, 16), :] = part
            y = tailp[kv].astype(F32)
            for h, part in enumerate(to_heads(y, tmp, heads)):
                e1[kv, h, pl.ds(0, 32), :] = part[:32]
                e2[kv, h, pl.ds(0, 48), :] = part[32:]

    near(0)

    def from_pair(r, _):
        b = me - 1 - 2 * r

        @pl.when(col == 0)
        def _():
            pair_copy(0, b).wait_recv()
            pair_copy(1, b).wait_recv()

        @pl.when(col == 1)
        def _():
            pair_copy(0, b).wait_recv()
        return 0

    lax.fori_loop(0, lev + col, from_pair, 0)

    def arrange(b, _):
        for kv in range(2):
            @pl.when(b < me)
            def _():
                x = far[kv, b].astype(F32)
                for h, part in enumerate(to_heads(x, tmp, heads)):
                    fk[kv, h, pl.ds(pl.multiple_of(b * own, own), own), :] = part

            @pl.when(b >= me)
            def _():
                for h in range(heads):
                    fk[kv, h, pl.ds(pl.multiple_of(b * own, own), own), :] = jnp.zeros((own, width), BF16)
        return 0

    chunks = (me + span - 1) // span
    lax.fori_loop(0, chunks * span, arrange, 0)
    wide = span * own

    def finish(h, _):
        for qd in range(rows // QUAD):
            limit = own * me + 32 * (qd - 1)
            for hf in range(2):
                at = qd * QUAD + hf * HALF
                q = eq[h, pl.ds(at, HALF), :]

                def chunk(c, state):
                    m, l, a = state
                    start = pl.multiple_of(c * wide, wide)
                    place = start + lax.broadcasted_iota(jnp.int32, (1, wide), 1)
                    s = lax.dot_general(q, fk[0, h, pl.ds(start, wide), :], (((1,), (1,)), ((), ())),
                                        preferred_element_type=F32)
                    s = s * gain + jnp.where(place < limit, 3.0, NEG)
                    fresh = jnp.maximum(m, jnp.max(s, axis=1, keepdims=True))
                    fade = jnp.exp2(m - fresh)
                    w = jnp.exp2(s - fresh)
                    l = l * fade + jnp.sum(w, axis=1, keepdims=True)
                    a = a * fade + jnp.dot(w.astype(BF16), fk[1, h, pl.ds(start, wide), :],
                                           preferred_element_type=F32)
                    return (fresh, l, a)

                state = (top[h, pl.ds(at, HALF), :], total[h, pl.ds(at, HALF), :],
                         acc[h, pl.ds(at, HALF), :])
                m, l, a = lax.fori_loop(0, chunks, chunk, state)
                acc[h, pl.ds(at, HALF), :] = a / l
        return 0

    lax.fori_loop(0, heads, finish, 0)
    for c in range(rows // HALF):
        for h in range(heads):
            otmp[pl.ds(h, HALF, stride=heads), :] = acc[h, pl.ds(c * HALF, HALF), :]
        o_ref[pl.ds(c * HALF, HALF)] = otmp[...].reshape(HALF, heads, width).astype(BF16)

    @pl.when(me < size - 1)
    def _():
        for kv in range(2):
            tail_copy(kv, 0, after).wait_send()
            tail_copy(kv, 1, after).wait_send()

    @pl.when(col == 0)
    def _():
        for kv in range(2):
            pair_copy(kv, me).wait_send()

    def sent(r, _):
        b = me - 2 * r

        @pl.when(climbs)
        def _():
            for kv in range(2):
                up_copy(kv, b, up).wait_send()

            @pl.when(col == 1)
            def _():
                up_copy(1, b - 1, up).wait_send()

        @pl.when(r > 0)
        def _():
            pair_copy(0, b).wait_send()

            @pl.when(col == 1)
            def _():
                pair_copy(1, b).wait_send()
        return 0

    lax.fori_loop(0, lev + 1, sent, 0)


def shards(size, queries, keys, values):
    rows, heads, width = queries.shape
    own = rows // 8
    span = max(n for n in range(1, min(size, 8) + 1) if size % n == 0)
    vmem = pl.BlockSpec(memory_space=pltpu.VMEM)
    return pl.pallas_call(
        functools.partial(kernel, size, span),
        out_shape=jax.ShapeDtypeStruct((rows, heads, width), BF16),
        in_specs=[vmem] * 3,
        out_specs=vmem,
        scratch_shapes=[
            pltpu.VMEM((2, size, own, heads, width), BF16),
            pltpu.VMEM((2, BLOCK, heads, width), BF16),
            pltpu.VMEM((2, 80, heads, width), BF16),
            pltpu.VMEM((2, 80, heads, width), BF16),
            pltpu.VMEM((heads, rows, width), BF16),
            pltpu.VMEM((2, heads, rows + BLOCK, width), BF16),
            pltpu.VMEM((2, heads, rows // 2, width), BF16),
            pltpu.VMEM((2, heads, rows // 4, width), BF16),
            pltpu.VMEM((2, heads, size * own, width), BF16),
            pltpu.VMEM((rows // HALF, HALF, NEAR), F32),
            pltpu.VMEM((heads, rows, width), F32),
            pltpu.VMEM((heads, rows, 1), F32),
            pltpu.VMEM((heads, rows, 1), F32),
            pltpu.VMEM((80 * heads, width), F32),
            pltpu.VMEM((HALF * heads, width), F32),
            pltpu.SemaphoreType.DMA((2, 2)),
            pltpu.SemaphoreType.DMA((2, 2)),
            pltpu.SemaphoreType.DMA((2, size)),
            pltpu.SemaphoreType.DMA((2, size)),
            pltpu.SemaphoreType.DMA((2, size)),
            pltpu.SemaphoreType.DMA((2, size)),
        ],
        compiler_params=pltpu.CompilerParams(
            collective_id=0, has_side_effects=True, vmem_limit_bytes=60 * 2**20),
    )(queries, keys, values)


def solution(mesh):
    spec = P(("groups", "seq"), "heads", None)
    return jax.shard_map(
        functools.partial(shards, mesh.shape["seq"]),
        mesh=mesh, in_specs=(spec,) * 3, out_specs=spec, check_vma=False)
```

time: 124 us -> 72.4 us (0.58)
  the two profiles are of different devices: /device:TPU:28 before, /device:TPU:30 now
where the time goes in v1:
time: 72.4 us; the launch traced here: 72.3 us
  Pallas kernels  70 us (97%)
  local copies, waits for them, and re-layouts  2.26 us (3%)
    pallas_call x1, Pallas kernels, shards(): pl.pallas_call(functools.partial(kernel, size, span), out_shape=jax.Shape...  70 us
    unnamed x1, local copies, waits for them, and re-layouts  2.26 us

profile of v1, /device:TPU:30, one launch (start us, length us, event | category | flops | bytes accessed | tf_op | source)
XLA Modules:
  0.0 72.3 jit_solution(12147960272639316725)
XLA Ops:
  0.0 70.0 %shard_map.37 = bf16[512,8,128]{2,1,0:T(8,128)(2,1)} custom-call(bf16[512,8,128]{2,1,0:T(8,128)(2,1)} %q_ref.1, bf16[512,8,128]{2,1,0:T(8,128)(2,1)} %k_ref.1, bf16[512,8,128]{2,1,0:T(8,128)(2,1)} %v_ref.1), custom_call_target="tpu_custom_call" | custom-call | tf_op jit(solution)/shard_map/pallas_call | solution.py:360
  70.0 2.3 %copy.5 = bf16[512,8,128]{2,1,0:T(8,128)(2,1)} copy(bf16[512,8,128]{2,1,0:T(8,128)(2,1)} %shard_map.37) | data formatting | bytes 2097152

commit v2 on v1

--- a/solution.py
+++ b/solution.py
@@ -40,6 +40,7 @@
     col = lax.rem(me, 2)
     lev = me // 2
     levels = size // 2
+    together = 2 - heads % 2
     pair = me + 1 - 2 * col
     sources = (k_ref, v_ref)
 
@@ -101,7 +102,7 @@
                 for h, part in enumerate(to_heads(four * 0.25, tmp, heads)):
                     e2[kv, h, pl.ds(BLOCK + c * 16, 16), :] = part
 
-    for kv in range(2):
+    for kv in (1, 0):
         for c in range(rows // BLOCK):
             split(kv, c)
 
@@ -109,19 +110,20 @@
     upper = jnp.minimum(size - 1 - me, 2)
     pl.semaphore_wait(barrier, lower + upper)
 
-    for kv in range(2):
+    for kv in (1, 0):
         @pl.when(climbs)
         def _():
             up_copy(kv, me, up).start()
 
-        @pl.when(me < size - 1)
-        def _():
+        @pl.when(col == 0)
+        def _():
+            pair_copy(kv, me).start()
+
+    @pl.when(me < size - 1)
+    def _():
+        for kv in range(2):
             tail_copy(kv, 0, after).start()
             tail_copy(kv, 1, after).start()
-
-        @pl.when(col == 0)
-        def _():
-            pair_copy(kv, me).start()
 
     for kv in range(2):
         for c in range(rows // BLOCK):
@@ -147,8 +149,9 @@
             bias[2 * qd + hf] = jnp.where(ok > 0, level, NEG)
 
     def near(qd):
-        def body(h, _):
-            for hf in range(2):
+        def body(g, _):
+            for part in range(2 * together):
+                h, hf = g * together + part // 2, part % 2
                 at = qd * QUAD + hf * HALF
                 q = eq[h, pl.ds(at, HALF), :]
                 kk, vv = (jnp.concatenate([
@@ -163,7 +166,7 @@
                 top[h, pl.ds(at, HALF), :] = m
                 acc[h, pl.ds(at, HALF), :] = jnp.dot(w.astype(BF16), vv, preferred_element_type=F32)
             return 0
-        lax.fori_loop(0, heads, body, 0)
+        lax.fori_loop(0, heads // together, body, 0)
 
     for qd in range(1, rows // QUAD):
         near(qd)
@@ -184,42 +187,29 @@
                 def _():
                     pair_copy(kv, b).start()
 
-        @pl.when(col == 1)
-        def _():
-            b = me + 1 - 2 * r
-
-            @pl.when(r == 1)
-            def _():
-                pair_copy(1, b).wait_recv()
-
-            @pl.when(r > 1)
-            def _():
-                up_copy(1, b, up).wait_recv()
-
-            @pl.when(climbs)
-            def _():
-                up_copy(1, b, up).start()
+        @pl.when((col == 1) & climbs)
+        def _():
+            even_on(r)
         return 0
 
-    def last_even():
-        @pl.when(col == 1)
-        def _():
-            b = me - 1 - 2 * lev
-
-            @pl.when(lev == 0)
-            def _():
-                pair_copy(1, b).wait_recv()
-
-            @pl.when(lev > 0)
-            def _():
-                up_copy(1, b, up).wait_recv()
-
-            @pl.when(climbs)
-            def _():
-                up_copy(1, b, up).start()
+    def even_on(r):
+        b = me + 1 - 2 * r
+
+        @pl.when(r == 1)
+        def _():
+            pair_copy(1, b).wait_recv()
+
+        @pl.when(r > 1)
+        def _():
+            up_copy(1, b, up).wait_recv()
+
+        up_copy(1, b, up).start()
 
     lax.fori_loop(1, lev + 1, pass_on, 0)
-    last_even()
+
+    @pl.when((col == 1) & climbs)
+    def _():
+        even_on(lev + 1)
 
     @pl.when(me == 0)
     def _():
@@ -250,71 +240,76 @@
 
     near(0)
 
-    def from_pair(r, _):
-        b = me - 1 - 2 * r
-
-        @pl.when(col == 0)
+    def arrange(s, _):
+        b = me - 1 - s
+        place = pl.multiple_of(s * own, own)
+        even = lax.rem(s, 2) == 0
+
+        @pl.when((s < me) & even)
         def _():
             pair_copy(0, b).wait_recv()
-            pair_copy(1, b).wait_recv()
-
-        @pl.when(col == 1)
-        def _():
-            pair_copy(0, b).wait_recv()
-        return 0
-
-    lax.fori_loop(0, lev + col, from_pair, 0)
-
-    def arrange(b, _):
-        for kv in range(2):
-            @pl.when(b < me)
-            def _():
+
+            @pl.when(col == 0)
+            def _():
+                pair_copy(1, b).wait_recv()
+
+            @pl.when((col == 1) & jnp.logical_not(climbs) & (s == 0))
+            def _():
+                pair_copy(1, b).wait_recv()
+
+            @pl.when((col == 1) & jnp.logical_not(climbs) & (s > 0))
+            def _():
+                up_copy(1, b, up).wait_recv()
+
+        @pl.when(s < me)
+        def _():
+            for kv in range(2):
                 x = far[kv, b].astype(F32)
                 for h, part in enumerate(to_heads(x, tmp, heads)):
-                    fk[kv, h, pl.ds(pl.multiple_of(b * own, own), own), :] = part
-
-            @pl.when(b >= me)
-            def _():
+                    fk[kv, h, pl.ds(place, own), :] = part
+
+        @pl.when(s >= me)
+        def _():
+            for kv in range(2):
                 for h in range(heads):
-                    fk[kv, h, pl.ds(pl.multiple_of(b * own, own), own), :] = jnp.zeros((own, width), BF16)
+                    fk[kv, h, pl.ds(place, own), :] = jnp.zeros((own, width), BF16)
         return 0
 
-    chunks = (me + span - 1) // span
-    lax.fori_loop(0, chunks * span, arrange, 0)
     wide = span * own
 
-    def finish(h, _):
-        for qd in range(rows // QUAD):
-            limit = own * me + 32 * (qd - 1)
-            for hf in range(2):
-                at = qd * QUAD + hf * HALF
-                q = eq[h, pl.ds(at, HALF), :]
-
-                def chunk(c, state):
-                    m, l, a = state
-                    start = pl.multiple_of(c * wide, wide)
-                    place = start + lax.broadcasted_iota(jnp.int32, (1, wide), 1)
-                    s = lax.dot_general(q, fk[0, h, pl.ds(start, wide), :], (((1,), (1,)), ((), ())),
-                                        preferred_element_type=F32)
-                    s = s * gain + jnp.where(place < limit, 3.0, NEG)
+    def chunk(c, _):
+        lax.fori_loop(c * span, (c + 1) * span, arrange, 0)
+        start = pl.multiple_of(c * wide, wide)
+        place = start + lax.broadcasted_iota(jnp.int32, (1, wide), 1)
+        known = jnp.where(place < own * me, 3.0, NEG)
+        masks = [jnp.where((place >= own // 2) & (place < own), NEG, known), known]
+
+        def body(h, _):
+            for qd in range(rows // QUAD):
+                for hf in range(2):
+                    at = qd * QUAD + hf * HALF
+                    m = top[h, pl.ds(at, HALF), :]
+                    s = lax.dot_general(eq[h, pl.ds(at, HALF), :], fk[0, h, pl.ds(start, wide), :],
+                                        (((1,), (1,)), ((), ())), preferred_element_type=F32)
+                    s = s * gain + masks[min(qd, 1)]
                     fresh = jnp.maximum(m, jnp.max(s, axis=1, keepdims=True))
                     fade = jnp.exp2(m - fresh)
                     w = jnp.exp2(s - fresh)
-                    l = l * fade + jnp.sum(w, axis=1, keepdims=True)
-                    a = a * fade + jnp.dot(w.astype(BF16), fk[1, h, pl.ds(start, wide), :],
-                                           preferred_element_type=F32)
-                    return (fresh, l, a)
-
-                state = (top[h, pl.ds(at, HALF), :], total[h, pl.ds(at, HALF), :],
-                         acc[h, pl.ds(at, HALF), :])
-                m, l, a = lax.fori_loop(0, chunks, chunk, state)
-                acc[h, pl.ds(at, HALF), :] = a / l
+                    top[h, pl.ds(at, HALF), :] = fresh
+                    total[h, pl.ds(at, HALF), :] = (
+                        total[h, pl.ds(at, HALF), :] * fade + jnp.sum(w, axis=1, keepdims=True))
+                    acc[h, pl.ds(at, HALF), :] = acc[h, pl.ds(at, HALF), :] * fade + jnp.dot(
+                        w.astype(BF16), fk[1, h, pl.ds(start, wide), :], preferred_element_type=F32)
+            return 0
+
+        lax.fori_loop(0, heads, body, 0)
         return 0
 
-    lax.fori_loop(0, heads, finish, 0)
+    lax.fori_loop(0, (me + span - 1) // span, chunk, 0)
     for c in range(rows // HALF):
         for h in range(heads):
-            otmp[pl.ds(h, HALF, stride=heads), :] = acc[h, pl.ds(c * HALF, HALF), :]
+            otmp[pl.ds(h, HALF, stride=heads), :] = (
+                acc[h, pl.ds(c * HALF, HALF), :] / total[h, pl.ds(c * HALF, HALF), :])
         o_ref[pl.ds(c * HALF, HALF)] = otmp[...].reshape(HALF, heads, width).astype(BF16)
 
     @pl.when(me < size - 1)
@@ -355,7 +350,7 @@
 def shards(size, queries, keys, values):
     rows, heads, width = queries.shape
     own = rows // 8
-    span = max(n for n in range(1, min(size, 8) + 1) if size % n == 0)
+    span = max(n for n in range(1, min(size, 4) + 1) if size % n == 0)
     vmem = pl.BlockSpec(memory_space=pltpu.VMEM)
     return pl.pallas_call(
         functools.partial(kernel, size, span),

time: 72.4 us -> 66.8 us (0.923)
  Pallas kernels: 70 us -> 64.4 us
    pallas_call x1, Pallas kernels: 70 us -> 64.4 us  [shards(): pl.pallas_call(functools.partial(kernel, size, span), out_shape=jax.Shape...]
where the time goes in v2:
time: 66.8 us; the launch traced here: 66.6 us
  Pallas kernels  64.4 us (96%)
  local copies, waits for them, and re-layouts  2.26 us (3%)
    pallas_call x1, Pallas kernels, shards(): pl.pallas_call(functools.partial(kernel, size, span), out_shape=jax.Shape...  64.4 us
    unnamed x1, local copies, waits for them, and re-layouts  2.26 us

profile of v2, /device:TPU:30, one launch (start us, length us, event | category | flops | bytes accessed | tf_op | source)
XLA Modules:
  0.0 66.6 jit_solution(14725812475682511294)
XLA Ops:
  0.0 64.4 %shard_map.37 = bf16[512,8,128]{2,1,0:T(8,128)(2,1)} custom-call(bf16[512,8,128]{2,1,0:T(8,128)(2,1)} %q_ref.1, bf16[512,8,128]{2,1,0:T(8,128)(2,1)} %k_ref.1, bf16[512,8,128]{2,1,0:T(8,128)(2,1)} %v_ref.1), custom_call_target="tpu_custom_call" | custom-call | tf_op jit(solution)/shard_map/pallas_call | solution.py:355
  64.4 2.3 %copy.5 = bf16[512,8,128]{2,1,0:T(8,128)(2,1)} copy(bf16[512,8,128]{2,1,0:T(8,128)(2,1)} %shard_map.37) | data formatting | bytes 2097152

commit v3 on v2

--- a/solution.py
+++ b/solution.py
@@ -27,6 +27,18 @@
     count, heads, width = values.shape
     pairs = values.reshape(count // 2, 2, heads, width)
     return pairs[:, 0] + pairs[:, 1]
+
+
+def across(column, count):
+    width = column.shape[1]
+    parts = [column] * (count // width)
+    if count % width:
+        parts.append(column[:, :count % width])
+    return jnp.concatenate(parts, 1) if len(parts) > 1 else parts[0]
+
+
+def with_ones(values):
+    return jnp.concatenate([values, jnp.ones_like(values)], 1)
 
 
 def kernel(size, span, q_ref, k_ref, v_ref, o_ref,
@@ -160,11 +172,12 @@
                     e2[kv, h, pl.ds(qd * BLOCK, BLOCK), :]], 0) for kv in range(2))
                 s = lax.dot_general(q, kk, (((1,), (1,)), ((), ())), preferred_element_type=F32)
                 s = s * gain + bias[2 * qd + hf]
-                m = jnp.max(s, axis=1, keepdims=True)
-                w = jnp.exp2(s - m)
-                total[h, pl.ds(at, HALF), :] = jnp.sum(w, axis=1, keepdims=True)
+                m = jnp.broadcast_to(jnp.max(s, axis=1, keepdims=True), (HALF, width))
+                w = jnp.exp2(s - across(m, NEAR)).astype(BF16)
+                both = jnp.dot(w, with_ones(vv), preferred_element_type=F32)
                 top[h, pl.ds(at, HALF), :] = m
-                acc[h, pl.ds(at, HALF), :] = jnp.dot(w.astype(BF16), vv, preferred_element_type=F32)
+                acc[h, pl.ds(at, HALF), :] = both[:, :width]
+                total[h, pl.ds(at, HALF), :] = both[:, width:]
             return 0
         lax.fori_loop(0, heads // together, body, 0)
 
@@ -294,12 +307,13 @@
                     s = s * gain + masks[min(qd, 1)]
                     fresh = jnp.maximum(m, jnp.max(s, axis=1, keepdims=True))
                     fade = jnp.exp2(m - fresh)
-                    w = jnp.exp2(s - fresh)
+                    w = jnp.exp2(s - across(fresh, wide)).astype(BF16)
+                    both = jnp.dot(w, with_ones(fk[1, h, pl.ds(start, wide), :]),
+                                   preferred_element_type=F32)
                     top[h, pl.ds(at, HALF), :] = fresh
+                    acc[h, pl.ds(at, HALF), :] = acc[h, pl.ds(at, HALF), :] * fade + both[:, :width]
                     total[h, pl.ds(at, HALF), :] = (
-                        total[h, pl.ds(at, HALF), :] * fade + jnp.sum(w, axis=1, keepdims=True))
-                    acc[h, pl.ds(at, HALF), :] = acc[h, pl.ds(at, HALF), :] * fade + jnp.dot(
-                        w.astype(BF16), fk[1, h, pl.ds(start, wide), :], preferred_element_type=F32)
+                        total[h, pl.ds(at, HALF), :] * fade + both[:, width:])
             return 0
 
         lax.fori_loop(0, heads, body, 0)
@@ -369,8 +383,8 @@
             pltpu.VMEM((2, heads, size * own, width), BF16),
             pltpu.VMEM((rows // HALF, HALF, NEAR), F32),
             pltpu.VMEM((heads, rows, width), F32),
-            pltpu.VMEM((heads, rows, 1), F32),
-            pltpu.VMEM((heads, rows, 1), F32),
+            pltpu.VMEM((heads, rows, width), F32),
+            pltpu.VMEM((heads, rows, width), F32),
             pltpu.VMEM((80 * heads, width), F32),
             pltpu.VMEM((HALF * heads, width), F32),
             pltpu.SemaphoreType.DMA((2, 2)),

time: 66.8 us -> 55.3 us (0.83)
  Pallas kernels: 64.4 us -> 52.9 us
    pallas_call x1, Pallas kernels: 64.4 us -> 52.9 us  [shards(): pl.pallas_call(functools.partial(kernel, size, span), out_shape=jax.Shape...]
where the time goes in v3:
time: 55.3 us; the launch traced here: 55.1 us
  Pallas kernels  52.9 us (96%)
  local copies, waits for them, and re-layouts  2.26 us (4%)
    pallas_call x1, Pallas kernels, shards(): pl.pallas_call(functools.partial(kernel, size, span), out_shape=jax.Shape...  52.9 us
    unnamed x1, local copies, waits for them, and re-layouts  2.26 us

profile of v3, /device:TPU:30, one launch (start us, length us, event | category | flops | bytes accessed | tf_op | source)
XLA Modules:
  0.0 55.1 jit_solution(4053679698139137119)
XLA Ops:
  0.0 52.9 %shard_map.37 = bf16[512,8,128]{2,1,0:T(8,128)(2,1)} custom-call(bf16[512,8,128]{2,1,0:T(8,128)(2,1)} %q_ref.1, bf16[512,8,128]{2,1,0:T(8,128)(2,1)} %k_ref.1, bf16[512,8,128]{2,1,0:T(8,128)(2,1)} %v_ref.1), custom_call_target="tpu_custom_call" | custom-call | tf_op jit(solution)/shard_map/pallas_call | solution.py:369
  52.9 2.3 %copy.5 = bf16[512,8,128]{2,1,0:T(8,128)(2,1)} copy(bf16[512,8,128]{2,1,0:T(8,128)(2,1)} %shard_map.37) | data formatting | bytes 2097152
